TPU v7x, 512 devices: a whole 4x4x16 slice. The times are simulated.
512 devices in a mesh: dom: 64 (over z, y), src: 4 (over x), rel: 2 (over core).
Axes of the slice: x: 4, y: 4, z: 16, core: 2. Of those that a mesh axis runs over, the one named last changes fastest.
Arguments:
- source_feats: bfloat16 [131072, 256], P(('dom', 'src', 'rel')), may hold values from -6 to 6
- rel_weight: bfloat16 [12, 256, 256], P('rel'), may hold values from -0.375 to 0.375
- halo_pick: int32 [64, 4, 2, 64], P('dom', 'src', 'rel'), may hold values from 0 to 1
- entry_index: int32 [64, 4, 2, 3, 64], P('dom', 'src', 'rel'), may hold values from 0 to 63, as said below
- entry_count: int32 [64, 4, 2], P('dom', 'src', 'rel'), may hold values from 1 to 64, as said below
- entry_values: bfloat16 [64, 4, 2, 64, 128, 128], P('dom', 'src', 'rel'), may hold values from -0.125 to 0.125
- cotangent: bfloat16 [131072, 256], P(('dom', 'src', 'rel')), may hold values from -0.0546875 to 0.0546875
Outputs:
- out_feats: bfloat16 [131072, 256], P(('dom', 'src', 'rel'))
- grad_rel: float32 [12, 256, 256], P('rel')
Inputs may be any that keep to these rules, and one draw needn't show every extreme that they name: `entry_index`: row 0 of an entry is a target block below 16, row 1 a partition below 64, row 2 a relation below 6. Over all 64 entries of one (p,s,g), every partition is named 64 // 64 times or once more. `entry_count`: live entries come first; some (p,s,g) has all 64 entries live in every draw.
All inputs are finite; a program needn't handle non-finite values.
Results may differ from a plain program's by a relative error of at most 0.0057.
Values may be sent and summed in bfloat16 or wider, within the bound.
A program may use at most 64 MiB of HBM per device.

v0:
```python
import jax
import jax.numpy as jnp
from jax import lax
from jax.sharding import PartitionSpec as P


def silu_slope(pre_values):
    logistic = jax.nn.sigmoid(pre_values)
    return logistic * (1.0 + pre_values * (1.0 - logistic))


def local(source_feats, rel_weight, halo_pick, entry_index, entry_count, entry_values, cotangent):
    partitions = lax.axis_size("dom")
    tile_rows = entry_values.shape[-1]
    features = source_feats.shape[1]
    chosen = halo_pick.reshape(-1)
    everyone = lax.all_gather(source_feats, "dom", axis=0, tiled=True)
    everyone = everyone.reshape(partitions, -1, tile_rows, features)
    halo_blocks = everyone[jnp.arange(partitions, dtype=jnp.int32), chosen]
    own_rows = cotangent.shape[0]
    tgt_blocks = own_rows * lax.axis_size("src") * lax.axis_size("rel") // tile_rows
    rel_local = rel_weight.shape[0]
    entry_table = entry_index.reshape(3, -1)
    slot_total = entry_table.shape[1]
    values = entry_values.reshape(-1, tile_rows, tile_rows)
    picked = halo_blocks[entry_table[1]]
    messages = jnp.einsum("eij,ejd->eid", values, picked, preferred_element_type=jnp.float32)
    live_mask = jnp.arange(slot_total, dtype=jnp.int32) < entry_count.reshape(())
    target_slot = entry_table[2] * tgt_blocks + entry_table[0]
    slot_numbers = jnp.arange(rel_local * tgt_blocks, dtype=jnp.int32)
    placement = ((slot_numbers[:, None] == target_slot[None, :]) & live_mask[None, :]).astype(
        jnp.float32
    )
    totals = jnp.einsum(
        "se,eid->sid",
        placement,
        messages,
        precision=lax.Precision.HIGHEST,
        preferred_element_type=jnp.float32,
    )
    relation_terms = totals.astype(jnp.bfloat16).reshape(
        rel_local, tgt_blocks * tile_rows, features
    )
    summed = lax.psum_scatter(
        jnp.einsum("rtd,rde->te", relation_terms, rel_weight, preferred_element_type=jnp.float32),
        ("src", "rel"),
        scatter_dimension=0,
        tiled=True,
    )
    out_feats = jax.nn.silu(summed).astype(jnp.bfloat16)
    local_grad = (cotangent.astype(jnp.float32) * silu_slope(summed)).astype(jnp.bfloat16)
    grad_rows = lax.all_gather(local_grad, ("src", "rel"), axis=0, tiled=True)
    weight_terms = jnp.einsum(
        "rtd,te->rde", relation_terms, grad_rows, preferred_element_type=jnp.float32
    )
    grad_rel = lax.psum(weight_terms, ("dom", "src"))
    return (out_feats, grad_rel)


def solution(mesh):
    return jax.shard_map(
        local,
        mesh=mesh,
        in_specs=(
            P(("dom", "src", "rel"), None),
            P("rel", None, None),
            P("dom", "src", "rel", None),
            P("dom", "src", "rel", None, None),
            P("dom", "src", "rel"),
            P("dom", "src", "rel", None, None, None),
            P(("dom", "src", "rel"), None),
        ),
        out_specs=(P(("dom", "src", "rel"), None), P("rel", None, None)),
        check_vma=False,
    )
```

profile of v0, /device:TPU:2, one launch (start us, length us, event | category | flops | bytes accessed | tf_op | source)
XLA Modules:
  0.0 711.4 jit_solution(15321850771566686382)
XLA Ops:
  7.2 0.0 copy-start
  7.2 0.0 all-gather.3.cloned.1.call-start
  7.2 0.7 all-gather.3.cloned.1.call-update
  7.9 0.0 reduce-scatter.2.cloned.1.call-start
  8.6 0.7 fusion.17
  9.3 0.7 add_bitcast_fusion
  10.0 0.7 fusion.18
  10.6 160.9 %all-gather.3.cloned.1.call-done = bf16[16384,256]{1,0:T(8,128)(2,1)} async-done(((bf16[256,256]{1,0:T(8,128)(2,1)}), bf16[16384,256]{1,0:T(8,128)(2,1)}) %all-gather.3.cloned.1.call-update) | async-done | bytes 8388624 | tf_op jit(solution)/shard_map/all_gather | solution.py:17
  171.5 6.2 gather_fusion
  177.7 4.9 gather_fusion.1
  182.6 0.0 copy-done
  182.6 6.7 fusion.5
  189.3 9.2 %copy.12 = f32[64,256,128]{1,0,2:T(8,128)} copy(f32[64,256,128]{2,1,0:T(8,128)} %fusion.5) | data formatting | bytes 16777216 | tf_op jit(solution)/shard_map/eij,ejd->eid/dot_general | solution.py:27
  198.5 8.4 %fusion.2 = bf16[96,128,256]{2,0,1:T(8,128)(2,1)S(1)} fusion(f32[64,256,128]{1,0,2:T(8,128)} %copy.12, s32[64]{0:T(128)S(1)} %add_bitcast_fusion, pred[64]{0:T(512)(128)(4,1)S(1)} %iota_compare_fusion.1), kind=kOutput, calls=%fused_computation.4 | convolution fusion | flops 2419077120 | bytes 14680384 | tf_op jit(solution)/shard_map/se,eid->sid/dot_general | solution.py:34
  207.0 0.0 copy-start.3
  207.0 3.7 copy.10
  210.6 0.0 copy-start.1
  210.6 2.6 copy-done.1
  213.3 0.0 copy-done.3
  213.3 0.0 copy-start.2
  213.3 3.3 convolution_bitcast_fusion
  216.5 0.0 reduce-scatter.2.cloned.1.call-update
  216.6 0.0 all-gather.5.cloned.1.call-start
  216.6 33.4 %reduce-scatter.2.cloned.1.call-done = f32[256,256]{1,0:T(8,128)} async-done(((f32[2048,256]{1,0:T(8,128)}), f32[256,256]{1,0:T(8,128)}) %reduce-scatter.2.cloned.1.call-update) | async-done | bytes 262160 | tf_op jit(solution)/shard_map/reduce_scatter | solution.py:44
  250.0 0.0 copy-done.2
  250.0 1.8 multiply_convert_fusion
  251.7 0.0 all-gather.5.cloned.1.call-update
  251.8 0.0 all-reduce.2.cloned.1.call-start
  251.8 32.6 %all-gather.5.cloned.1.call-done = bf16[2048,256]{1,0:T(8,128)(2,1)} async-done(((bf16[256,256]{1,0:T(8,128)(2,1)}), bf16[2048,256]{1,0:T(8,128)(2,1)}) %all-gather.5.cloned.1.call-update) | async-done | bytes 1048592 | tf_op jit(solution)/shard_map/all_gather | solution.py:52
  284.4 6.0 fusion.7
  290.4 0.0 all-reduce.2.cloned.1.call-update
  290.4 411.6 %all-reduce.2.cloned.1.call-done = f32[6,256,256]{2,1,0:T(8,128)} async-done(((f32[6,256,256]{2,1,0:T(8,128)}), f32[6,256,256]{2,1,0:T(8,128)}) %all-reduce.2.cloned.1.call-update) | async-done | bytes 1572880 | tf_op jit(solution)/shard_map/psum | solution.py:56
  702.1 2.7 copy.16
  (2 shorter events, 0.0 us)
Async XLA Ops:
  7.2 175.5 %copy-start = (bf16[1,1,1,64,128,128]{5,4,3,2,1,0:T(8,128)(2,1)S(1)}, bf16[1,1,1,64,128,128]{5,4,3,2,1,0:T(8,128)(2,1)}, u32[]{:S(2)}) copy-start(bf16[1,1,1,64,128,128]{5,4,3,2,1,0:T(8,128)(2,1)} %param.12) | copy-start | bytes 6291460
  7.2 164.4 %all-gather.3.cloned.1.call-start = ((), (), s32[]{:S(2)}) async-start(), calls=%async_computation.1 | async-start | bytes 8519680 | tf_op jit(solution)/shard_map/all_gather | solution.py:17
  7.9 242.1 %reduce-scatter.2.cloned.1.call-start = ((), (), s32[]{:S(2)}) async-start(), calls=%async_computation.2 | async-start | bytes 2359296 | tf_op jit(solution)/shard_map/reduce_scatter | solution.py:44
  207.0 6.3 copy-start.3
  210.6 2.7 copy-start.1
  213.3 36.7 %copy-start.2 = (bf16[256,256]{1,0:T(8,128)(2,1)S(1)}, bf16[256,256]{1,0:T(8,128)(2,1)}, u32[]{:S(2)}) copy-start(bf16[256,256]{1,0:T(8,128)(2,1)} %param.13) | copy-start | bytes 393220
  216.6 67.8 %all-gather.5.cloned.1.call-start = ((), (), s32[]{:S(2)}) async-start(), calls=%async_computation.3 | async-start | bytes 1179648 | tf_op jit(solution)/shard_map/all_gather | solution.py:52
  251.8 450.3 %all-reduce.2.cloned.1.call-start = ((), (), s32[]{:S(2)}) async-start(), calls=%async_computation.4 | async-start | bytes 3145728 | tf_op jit(solution)/shard_map/psum | solution.py:56
Sparse Core Ops, SparseCore 0:
  10.9 160.5 all-gather.2
  216.7 33.2 reduce-scatter.1
  252.7 31.6 all-gather.4
  290.6 411.4 all-reduce.1
where the time goes:
time: 712 us; the launch traced here: 711 us
  waiting for transfers between devices  639 us (90%)
  local copies, waits for them, and re-layouts  29.3 us (4%)
  matrix products  24.4 us (3%)
  between operations  14.5 us (2%)
    psum x1, waiting for transfers between devices, local(): grad_rel = lax.psum(weight_terms, ('dom', 'src'))  412 us
    all_gather x1, waiting for transfers between devices, local(): everyone = lax.all_gather(source_feats, 'dom', axis=0, tiled=True)  161 us
    reduce_scatter x1, waiting for transfers between devices, local(): lax.psum_scatter(jnp.einsum('rtd,rde->te', relation_terms, rel_weight, pr...  33.4 us
    all_gather x1, waiting for transfers between devices, local(): grad_rows = lax.all_gather(local_grad, ('src', 'rel'), axis=0, tiled=True)  32.6 us
  transfers between devices with their start and end apart: 4, of which 4 were waited for; matrix products, arithmetic and copies ran while one was open for 0% of the time, Pallas kernels for 0%

commit v1 on v0

v1 whole, which is shorter than its diff:
```python
import jax
import jax.numpy as jnp
from jax import lax
from jax.experimental import pallas as pl
from jax.experimental.pallas import tpu as pltpu
from jax.sharding import PartitionSpec as P

MESH = pl.DeviceIdType.MESH
F32 = jnp.float32
BF16 = jnp.bfloat16

NY = 4
NZ = 16
NX = 4
BLOCK = 128
D = 256
REL = 6
CHUNKS = 8
ROWS_P = 160
HALF_P = 80
ROWS_Q = 96
HALF_Q = 48


def remote(src, dst, send_sem, recv_sem, to):
    return pltpu.make_async_remote_copy(
        src_ref=src, dst_ref=dst, send_sem=send_sem, recv_sem=recv_sem,
        device_id=to, device_id_type=MESH)


def signal_all(targets):
    barrier = pltpu.get_barrier_semaphore()
    for to in targets:
        pl.semaphore_signal(barrier, inc=1, device_id=to, device_id_type=MESH)
    pl.semaphore_wait(barrier, len(targets))


def gather_kernel(src, out, own_sem, pf_s, pf_r, pb_s, pb_r, yf_s, yf_r, yb_s, yb_r,
                  ff_s, ff_r, fb_s, fb_r, q0_s, q0_r, qf_s, qf_r, qb_s, qb_r):
    dom = lax.axis_index("dom")
    z, y = dom // NY, dom % NY

    def at(zo, yo):
        return ((z + zo + NZ) % NZ) * NY + (y + yo + NY) % NY

    z_up, z_down = {"dom": at(1, 0)}, {"dom": at(-1, 0)}
    y_up, y_down, y_far = {"dom": at(0, 1)}, {"dom": at(0, -1)}, {"dom": at(0, 2)}
    signal_all([z_up, z_down, y_up, y_down, y_far])

    sent = []

    def send(where, row, count, s, r, to):
        index = at(*where)
        own = where == (0, 0)
        source = src.at[pl.ds(row, count)] if own else out.at[index, pl.ds(row, count)]
        copy = remote(source, out.at[index, pl.ds(row, count)], s, r, to)
        copy.start()
        sent.append(copy)

    def arrive(where, row, count, s, r):
        index = at(*where)
        ref = out.at[index, pl.ds(row, count)]
        remote(ref, ref, s, r, z_up).wait_recv()

    own_copy = pltpu.make_async_copy(src, out.at[dom], own_sem)

    def p_step(k):
        lo, n = (0, ROWS_P) if k < NZ // 2 else (0, HALF_P)
        send((-(k - 1), 0), lo, n, pf_s.at[k], pf_r.at[k], z_up)
        lo, n = (0, ROWS_P) if k < NZ // 2 else (HALF_P, HALF_P)
        send((k - 1, 0), lo, n, pb_s.at[k], pb_r.at[k], z_down)

    def p_arrive(k):
        lo, n = (0, ROWS_P) if k < NZ // 2 else (0, HALF_P)
        arrive((-k, 0), lo, n, pf_s.at[k], pf_r.at[k])
        lo, n = (0, ROWS_P) if k < NZ // 2 else (HALF_P, HALF_P)
        arrive((k, 0), lo, n, pb_s.at[k], pb_r.at[k])

    def q_step(k, m):
        lo, n = (ROWS_P, ROWS_Q) if k < NZ // 2 else (ROWS_P, HALF_Q)
        send((-(k - 1), m), lo, n, qf_s.at[k, m], qf_r.at[k, m], z_up)
        lo, n = (ROWS_P, ROWS_Q) if k < NZ // 2 else (ROWS_P + HALF_Q, HALF_Q)
        send((k - 1, m), lo, n, qb_s.at[k, m], qb_r.at[k, m], z_down)

    def q_arrive(k, m):
        lo, n = (ROWS_P, ROWS_Q) if k < NZ // 2 else (ROWS_P, HALF_Q)
        arrive((-k, m), lo, n, qf_s.at[k, m], qf_r.at[k, m])
        lo, n = (ROWS_P, ROWS_Q) if k < NZ // 2 else (ROWS_P + HALF_Q, HALF_Q)
        arrive((k, m), lo, n, qb_s.at[k, m], qb_r.at[k, m])

    def offsets(k):
        if k == 0:
            return [(0, 0)]
        if k == NZ // 2:
            return [(2 * k - 1, k)]
        return [(2 * k - 1, -k), (2 * k, k)]

    def y_step(k):
        for j, zo in offsets(k):
            send((zo, 0), 0, ROWS_P, yf_s.at[j], yf_r.at[j], y_up)
            send((zo, 0), 0, ROWS_P, yb_s.at[j], yb_r.at[j], y_down)

    def y_forward(k):
        for j, zo in offsets(k):
            arrive((zo, -1), 0, ROWS_P, yf_s.at[j], yf_r.at[j])
            send((zo, -1), 0, HALF_P, ff_s.at[j], ff_r.at[j], y_up)
            arrive((zo, 1), 0, ROWS_P, yb_s.at[j], yb_r.at[j])
            send((zo, 1), HALF_P, HALF_P, fb_s.at[j], fb_r.at[j], y_down)

    p_step(1)
    send((0, 0), ROWS_P, ROWS_Q, q0_s.at[0], q0_r.at[0], y_up)
    send((0, 0), ROWS_P, ROWS_Q, q0_s.at[1], q0_r.at[1], y_down)
    send((0, 0), ROWS_P, ROWS_Q, q0_s.at[2], q0_r.at[2], y_far)
    q_step(1, 0)
    y_step(0)
    own_copy.start()
    arrive((0, -1), ROWS_P, ROWS_Q, q0_s.at[0], q0_r.at[0])
    q_step(1, 3)
    arrive((0, 1), ROWS_P, ROWS_Q, q0_s.at[1], q0_r.at[1])
    q_step(1, 1)
    arrive((0, 2), ROWS_P, ROWS_Q, q0_s.at[2], q0_r.at[2])
    q_step(1, 2)
    for k in range(1, NZ // 2 + 1):
        p_arrive(k)
        if k < NZ // 2:
            p_step(k + 1)
        y_step(k)
        y_forward(k - 1)
        for m in (0, 3, 1, 2):
            q_arrive(k, m)
            if k < NZ // 2:
                q_step(k + 1, m)
    y_forward(NZ // 2)
    for k in range(NZ // 2 + 1):
        for j, zo in offsets(k):
            arrive((zo, 2), 0, HALF_P, ff_s.at[j], ff_r.at[j])
            arrive((zo, 2), HALF_P, HALF_P, fb_s.at[j], fb_r.at[j])
    for copy in sent:
        copy.wait_send()
    own_copy.wait()


def gather_sources(source_feats):
    rows = source_feats.shape[0]
    dma = pltpu.SemaphoreType.DMA
    steps = NZ // 2 + 1
    return pl.pallas_call(
        gather_kernel,
        out_shape=jax.ShapeDtypeStruct((NZ * NY, rows, D), BF16),
        in_specs=[pl.BlockSpec(memory_space=pltpu.VMEM)],
        out_specs=pl.BlockSpec(memory_space=pl.ANY),
        scratch_shapes=[dma] + [dma((steps,))] * 4 + [dma((NZ,))] * 8
        + [dma((3,))] * 2 + [dma((steps, NY))] * 4,
        compiler_params=pltpu.CompilerParams(collective_id=0, has_side_effects=True),
        name="gather_sources",
    )(source_feats)


def message_kernel(pick, table, count, blocks, values, weight, terms_out, pre_out,
                   held, total, terms, held_sem, terms_sem):
    live = count[0]

    def fetch(e):
        q = table[1, e]
        return pltpu.make_async_copy(blocks.at[2 * q + pick[q]], held.at[e], held_sem.at[e])

    def start(e, carry):
        fetch(e).start()
        return carry

    lax.fori_loop(0, live, start, 0)

    def clear(i, carry):
        total[i] = jnp.zeros((BLOCK, D), F32)
        return carry

    lax.fori_loop(0, CHUNKS * REL * 2, clear, 0)

    def step(e, carry):
        fetch(e).wait()
        message = jnp.dot(values[e], held[e], preferred_element_type=F32)
        target = table[0, e]
        slot = (target // 2 * REL + table[2, e]) * 2 + target % 2
        total[slot] = total[slot] + message
        return carry

    lax.fori_loop(0, live, step, 0)

    def flush(c):
        return pltpu.make_async_copy(terms.at[c], terms_out.at[c], terms_sem.at[c])

    def project(c, carry):
        for r in range(REL):
            for h in range(2):
                terms[c, r, pl.ds(h * BLOCK, BLOCK)] = total[(c * REL + r) * 2 + h].astype(BF16)
        flush(c).start()
        value = jnp.dot(terms[c, 0], weight[0], preferred_element_type=F32)
        for r in range(1, REL):
            value = value + jnp.dot(terms[c, r], weight[r], preferred_element_type=F32)
        pre_out[c] = value
        return carry

    lax.fori_loop(0, CHUNKS, project, 0)
    for c in range(CHUNKS):
        flush(c).wait()


def messages(pick, table, count, blocks, values, weight):
    smem = pl.BlockSpec(memory_space=pltpu.SMEM)
    vmem = pl.BlockSpec(memory_space=pltpu.VMEM)
    entries = values.shape[0]
    return pl.pallas_call(
        message_kernel,
        out_shape=(jax.ShapeDtypeStruct((CHUNKS, REL, 2 * BLOCK, D), BF16),
                   jax.ShapeDtypeStruct((CHUNKS, 2 * BLOCK, D), F32)),
        in_specs=[smem, smem, smem, pl.BlockSpec(memory_space=pl.ANY), vmem, vmem],
        out_specs=(pl.BlockSpec(memory_space=pl.ANY), vmem),
        scratch_shapes=[
            pltpu.VMEM((entries, BLOCK, D), BF16),
            pltpu.VMEM((CHUNKS * REL * 2, BLOCK, D), F32),
            pltpu.VMEM((CHUNKS, REL, 2 * BLOCK, D), BF16),
            pltpu.SemaphoreType.DMA((entries,)),
            pltpu.SemaphoreType.DMA((CHUNKS,)),
        ],
        compiler_params=pltpu.CompilerParams(vmem_limit_bytes=56 << 20),
        name="messages",
    )(pick, table, count, blocks, values, weight)


def reduce_kernel(pre, terms_hbm, cot, out, grad,
                  ex, cs, cr, rows, terms, acc,
                  a_send, a_recv, b_send, b_recv, a_sum, b_sum,
                  a2_send, a2_recv, b2_send, b2_recv, tail, z_send, z_recv, z_full,
                  a_all, b_all,
                  t_sem, ex_s, ex_r, cx_s, cx_r, gx_s, gx_r, gp_s, gp_r,
                  s1_s, s1_r, s2_s, s2_r, z1_s, z1_r, z2_s, z2_r, s4_s, s4_r, s5_s, s5_r):
    dom, s, g = lax.axis_index("dom"), lax.axis_index("src"), lax.axis_index("rel")
    z, y = dom // NY, dom % NY
    partner = {"rel": 1 - g}

    def x_peer(d):
        return {"src": (s + d) % NX}

    def y_peer(d):
        return {"dom": z * NY + (y + d) % NY}

    def z_peer(d):
        return {"dom": ((z + d) % NZ) * NY + y}

    signal_all([partner] + [x_peer(d) for d in range(1, NX)]
               + [y_peer(d) for d in range(1, NY)] + [z_peer(d) for d in range(1, NZ)])

    sent = []

    def go(copy):
        copy.start()
        sent.append(copy)
        return copy

    swaps = {}
    for i in (1, 2, 3, 0):
        sp = (s + i) % NX
        swaps[i] = go(remote(pre.at[sp * 2 + (1 - g)], ex.at[sp], ex_s.at[i], ex_r.at[i], partner))
    load = pltpu.make_async_copy(terms_hbm, terms, t_sem)
    load.start()
    z_send[...] = jnp.zeros_like(z_send)

    moves = {}
    for i in (1, 2, 3):
        sp = (s + i) % NX
        swaps[i].wait_recv()
        for b in range(8):
            part = pl.ds(b * 32, 32)
            cs[i - 1, part] = (pre[sp * 2 + g, part] + ex[sp, part]).astype(BF16)
        moves[i] = go(remote(cs.at[i - 1], cr.at[i - 1], cx_s.at[i - 1], cx_r.at[i - 1], x_peer(i)))
    swaps[0].wait_recv()
    for i in (1, 2, 3):
        moves[i].wait_recv()
    own = s * 2 + g
    for b in range(8):
        part = pl.ds(b * 32, 32)
        value = pre[own, part] + ex[s, part]
        for i in range(3):
            value = value + cr[i, part].astype(F32)
        logistic = 1.0 / (1.0 + jnp.exp(-value))
        out[part] = (value * logistic).astype(BF16)
        slope = logistic * (1.0 + value * (1.0 - logistic))
        rows[own, part] = (cot[part].astype(F32) * slope).astype(BF16)

    gx = {}
    for d in (1, 2, 3):
        gx[d] = go(remote(rows.at[own], rows.at[own], gx_s.at[d], gx_r.at[d], x_peer(d)))
    gp = {0: go(remote(rows.at[own], rows.at[own], gp_s.at[0], gp_r.at[0], partner))}

    def add_terms(c, first=False):
        def one(r, carry):
            product = lax.dot_general(terms[c, r], rows[c], (((0,), (0,)), ((), ())),
                                      preferred_element_type=F32)
            if first:
                acc[r] = product
            else:
                acc[r] = acc[r] + product
            return carry

        lax.fori_loop(0, REL, one, 0)

    load.wait()
    add_terms(own, first=True)
    gp[0].wait_recv()
    add_terms(s * 2 + 1 - g)
    for d in (1, 2, 3):
        gx[d].wait_recv()
        c = (s - d + NX) % NX * 2 + g
        gp[d] = go(remote(rows.at[c], rows.at[c], gp_s.at[d], gp_r.at[d], partner))
        add_terms(c)
    for d in (1, 2, 3):
        gp[d].wait_recv()
        add_terms((s - d + NX) % NX * 2 + 1 - g)

    first_a, first_b = {}, {}
    for d in (1, 2, 3):
        xp, yp = (s + d) % NX, (y + d) % NY
        for r in range(3):
            a_send[d - 1, r] = acc[r, pl.ds(xp * 64, 64)].astype(BF16)
        first_a[d] = go(remote(a_send.at[d - 1], a_recv.at[d - 1], s1_s.at[0, d], s1_r.at[0, d], x_peer(d)))
        for r in range(3):
            b_send[d - 1, r] = acc[3 + r, pl.ds(yp * 64, 64)].astype(BF16)
        first_b[d] = go(remote(b_send.at[d - 1], b_recv.at[d - 1], s1_s.at[1, d], s1_r.at[1, d], y_peer(d)))
    for d in (1, 2, 3):
        first_a[d].wait_recv()
        first_b[d].wait_recv()
    for r in range(3):
        value = acc[r, pl.ds(s * 64, 64)]
        for i in range(3):
            value = value + a_recv[i, r].astype(F32)
        a_sum[r] = value
        value = acc[3 + r, pl.ds(y * 64, 64)]
        for i in range(3):
            value = value + b_recv[i, r].astype(F32)
        b_sum[r] = value
    second_a, second_b = {}, {}
    for d in (1, 2, 3):
        xp, yp = (s + d) % NX, (y + d) % NY
        for r in range(3):
            a2_send[d - 1, r] = a_sum[r, pl.ds(yp * 16, 16)].astype(BF16)
        second_a[d] = go(remote(a2_send.at[d - 1], a2_recv.at[d - 1], s2_s.at[0, d], s2_r.at[0, d], y_peer(d)))
        for r in range(3):
            b2_send[d - 1, r] = b_sum[r, pl.ds(xp * 16, 16)].astype(BF16)
        second_b[d] = go(remote(b2_send.at[d - 1], b2_recv.at[d - 1], s2_s.at[1, d], s2_r.at[1, d], x_peer(d)))
    for d in (1, 2, 3):
        second_a[d].wait_recv()
        second_b[d].wait_recv()
    for r in range(3):
        value = a_sum[r, pl.ds(y * 16, 16)]
        for i in range(3):
            value = value + a2_recv[i, r].astype(F32)
        tail[r] = value
        value = b_sum[r, pl.ds(s * 16, 16)]
        for i in range(3):
            value = value + b2_recv[i, r].astype(F32)
        tail[3 + r] = value
    for j in range(NZ):
        for r in range(REL):
            z_send[j, pl.ds(r, 1)] = tail[r, pl.ds(j, 1)]
    third = []
    for d in range(1, NZ):
        third.append(go(remote(z_send.at[(z + d) % NZ], z_recv.at[d], z1_s.at[d], z1_r.at[d], z_peer(d))))
    value = z_send[z]
    for d in range(1, NZ):
        third[d - 1].wait_recv()
        value = value + z_recv[d]
    z_full[z] = value

    fourth = []
    for d in range(1, NZ):
        fourth.append(go(remote(z_full.at[z], z_full.at[z], z2_s.at[d], z2_r.at[d], z_peer(d))))
    for copy in fourth:
        copy.wait_recv()
    for j in range(NZ):
        for r in range(REL):
            tail[r, pl.ds(j, 1)] = z_full[j, pl.ds(r, 1)]
    for r in range(3):
        a_all[s, y, r] = tail[r].astype(BF16)
        b_all[y, s, r] = tail[3 + r].astype(BF16)
    fifth = []
    for d in (1, 2, 3):
        fifth.append(go(remote(a_all.at[s, y], a_all.at[s, y], s4_s.at[0, d], s4_r.at[0, d], y_peer(d))))
        fifth.append(go(remote(b_all.at[y, s], b_all.at[y, s], s4_s.at[1, d], s4_r.at[1, d], x_peer(d))))
    for copy in fifth:
        copy.wait_recv()
    sixth = []
    for d in (1, 2, 3):
        sixth.append(go(remote(a_all.at[s], a_all.at[s], s5_s.at[0, d], s5_r.at[0, d], x_peer(d))))
        sixth.append(go(remote(b_all.at[y], b_all.at[y], s5_s.at[1, d], s5_r.at[1, d], y_peer(d))))
    for copy in sixth:
        copy.wait_recv()
    for i in range(4):
        for j in range(4):
            for r in range(3):
                part = pl.ds(64 * i + 16 * j, 16)
                grad[r, part] = a_all[i, j, r].astype(F32)
                grad[3 + r, part] = b_all[i, j, r].astype(F32)
    for copy in sent:
        copy.wait_send()


def reduce_and_grad(pre, terms, cotangent):
    vmem = pl.BlockSpec(memory_space=pltpu.VMEM)
    dma = pltpu.SemaphoreType.DMA
    V = pltpu.VMEM
    return pl.pallas_call(
        reduce_kernel,
        out_shape=(jax.ShapeDtypeStruct((2 * BLOCK, D), BF16),
                   jax.ShapeDtypeStruct((REL, D, D), F32)),
        in_specs=[vmem, pl.BlockSpec(memory_space=pl.ANY), vmem],
        out_specs=(vmem, vmem),
        scratch_shapes=[
            V((NX, 256, D), F32), V((3, 256, D), BF16), V((3, 256, D), BF16),
            V((CHUNKS, 256, D), BF16), V((CHUNKS, REL, 256, D), BF16), V((REL, D, D), F32),
            V((3, 3, 64, D), BF16), V((3, 3, 64, D), BF16), V((3, 3, 64, D), BF16), V((3, 3, 64, D), BF16),
            V((3, 64, D), F32), V((3, 64, D), F32),
            V((3, 3, 16, D), BF16), V((3, 3, 16, D), BF16), V((3, 3, 16, D), BF16), V((3, 3, 16, D), BF16),
            V((REL, 16, D), F32), V((NZ, 8, D), F32), V((NZ, 8, D), F32), V((NZ, 8, D), F32),
            V((4, 4, 3, 16, D), BF16), V((4, 4, 3, 16, D), BF16),
            dma, dma((4,)), dma((4,)), dma((3,)), dma((3,)), dma((4,)), dma((4,)), dma((4,)), dma((4,)),
            dma((2, 4)), dma((2, 4)), dma((2, 4)), dma((2, 4)), dma((NZ,)), dma((NZ,)), dma((NZ,)), dma((NZ,)),
            dma((2, 4)), dma((2, 4)), dma((2, 4)), dma((2, 4)),
        ],
        compiler_params=pltpu.CompilerParams(
            collective_id=1, has_side_effects=True, vmem_limit_bytes=56 << 20),
        name="reduce_and_grad",
    )(pre, terms, cotangent)


def local(source_feats, rel_weight, halo_pick, entry_index, entry_count, entry_values, cotangent):
    slots = entry_index.shape[-1]
    gathered = gather_sources(source_feats)
    terms, pre = messages(
        halo_pick.reshape(-1), entry_index.reshape(3, slots), entry_count.reshape(1),
        gathered.reshape(-1, BLOCK, D), entry_values.reshape(slots, BLOCK, BLOCK), rel_weight)
    return reduce_and_grad(pre, terms, cotangent)


def solution(mesh):
    return jax.shard_map(
        local,
        mesh=mesh,
        in_specs=(
            P(("dom", "src", "rel"), None),
            P("rel", None, None),
            P("dom", "src", "rel", None),
            P("dom", "src", "rel", None, None),
            P("dom", "src", "rel"),
            P("dom", "src", "rel", None, None, None),
            P(("dom", "src", "rel"), None),
        ),
        out_specs=(P(("dom", "src", "rel"), None), P("rel", None, None)),
        check_vma=False,
    )
```

time: 712 us -> 171 us (0.24)
  the two profiles are of different devices: /device:TPU:2 before, /device:TPU:8 now
where the time goes in v1:
time: 171 us; the launch traced here: 172 us
  Pallas kernels  165 us (96%)
  local copies, waits for them, and re-layouts  5.56 us (3%)
    pallas_call x1, Pallas kernels, reduce_and_grad(): pl.pallas_call(reduce_kernel, out_shape=(jax.ShapeDtypeStruct((2 * BLOCK,...  78 us
    pallas_call x1, Pallas kernels, gather_sources(): pl.pallas_call(gather_kernel, out_shape=jax.ShapeDtypeStruct((NZ * NY, ro...  69.1 us
    pallas_call x1, Pallas kernels, messages(): pl.pallas_call(message_kernel, out_shape=(jax.ShapeDtypeStruct((CHUNKS, R...  17.6 us
    unnamed x3, local copies, waits for them, and re-layouts  5.56 us

profile of v1, /device:TPU:8, one launch (start us, length us, event | category | flops | bytes accessed | tf_op | source)
XLA Modules:
  0.0 171.6 jit_solution(383258063772241355)
XLA Ops:
  1.3 1.3 copy.11
  2.5 69.1 %gather_sources.1 = bf16[64,256,256]{2,1,0:T(8,128)(2,1)} custom-call(bf16[256,256]{1,0:T(8,128)(2,1)} %src.1), custom_call_target="tpu_custom_call" | custom-call | tf_op jit(solution)/shard_map/gather_sources/pallas_call | solution.py:147
  71.6 17.6 %messages.1 = (bf16[8,6,256,256]{3,2,1,0:T(8,128)(2,1)}, f32[8,256,256]{2,1,0:T(8,128)}) custom-call(s32[64]{0:T(128)} %bitcast.11, s32[3,64]{1,0:T(4,128)} %bitcast.10, s32[1]{0:T(128)} %bitcast.7.count, bf16[128,128,256]{2,1,0:T(8,128)(2,1)} %bitcast.8, bf16[64,128,128]{2,1,0:T(8,128)(2,1)} %bitcast.9, bf16[6,256,256]{2,1,0:T(8,128)(2,1)} %weight.1), custom_call_target="tpu_custom_call" | custom-call | tf_op jit(solution)/shard_map/messages/pallas_call | solution.py:212
  89.3 78.0 %reduce_and_grad.1 = (bf16[256,256]{1,0:T(8,128)(2,1)}, f32[6,256,256]{2,1,0:T(8,128)}) custom-call(f32[8,256,256]{2,1,0:T(8,128)} %get-tuple-element.4.pre, bf16[8,6,256,256]{3,2,1,0:T(8,128)(2,1)} %get-tuple-element.5.terms_hbm, bf16[256,256]{1,0:T(8,128)(2,1)} %cot.1), custom_call_target="tpu_custom_call" | custom-call | tf_op jit(solution)/shard_map/reduce_and_grad/pallas_call | solution.py:411
  167.3 1.6 copy.15
  168.8 2.7 %copy.16 = f32[6,256,256]{2,1,0:T(8,128)} copy(f32[6,256,256]{2,1,0:T(8,128)} %get-tuple-element.9) | data formatting | bytes 3145728

commit v2 on v0

v2 whole, which is shorter than its diff:
```python
import jax
import jax.numpy as jnp
from jax import lax
from jax.experimental import pallas as pl
from jax.experimental.pallas import tpu as pltpu
from jax.sharding import PartitionSpec as P

MESH = pl.DeviceIdType.MESH
F32 = jnp.float32
BF16 = jnp.bfloat16
I32 = jnp.int32

NY = 4
NZ = 16
NX = 4
PARTS = 64
BLOCK = 128
D = 256
REL = 6
CHUNKS = 8
SLOTS = CHUNKS * REL * 2
ROWS_P = 160
HALF_P = 80
ROWS_Q = 96
HALF_Q = 48
FAR = NZ // 2

TIME_P = [0.0] + [4.0 * k for k in range(1, 9)]
TIME_Y = [3.0, 8.0, 13.2, 18.5, 24.0, 29.0, 34.5, 39.7, 44.0]
TIME_Q = [0.0, 7.5, 15.0, 22.5, 30.0, 35.0, 39.0, 43.0, 45.0]


def remote(src, dst, send_sem, recv_sem, to):
    return pltpu.make_async_remote_copy(
        src_ref=src, dst_ref=dst, send_sem=send_sem, recv_sem=recv_sem,
        device_id=to, device_id_type=MESH)


def offsets(k):
    if k == 0:
        return [(0, 0)]
    if k == FAR:
        return [(2 * k - 1, k)]
    return [(2 * k - 1, -k), (2 * k, k)]


def layer_kernel(src, table, pick, count, values_hbm, weight_hbm, cot,
                 out, a_out, b_out,
                 held, values, weight, chain, tab, tab_s, terms, work, keep, give, ex, cs, cr, rows, acc,
                 result, a_all, b_all,
                 a_send, a_recv, b_send, b_recv, a_sum, b_sum,
                 a2_send, a2_recv, b2_send, b2_recv, tail, z_rows, z_send, z_recv, z_full,
                 own_sem, val_sem, w_sem, tab_sem, out_sem,
                 pf_s, pf_r, pb_s, pb_r, yf_s, yf_r, yb_s, yb_r,
                 ff_s, ff_r, fb_s, fb_r, q0_s, q0_r, qf_s, qf_r, qb_s, qb_r,
                 ex_s, ex_r, cx_s, cx_r, gx_s, gx_r, gp_s, gp_r,
                 s1_s, s1_r, s2_s, s2_r, z1_s, z1_r, z2_s, z2_r, s4_s, s4_r, s5_s, s5_r):
    dom, s, g = lax.axis_index("dom"), lax.axis_index("src"), lax.axis_index("rel")
    z, y = dom // NY, dom % NY
    turn = 1 - 2 * g
    partner = {"rel": 1 - g}

    def at(zo, yo):
        return ((z + zo + NZ) % NZ) * NY + (y + yo + NY) % NY

    def x_at(o):
        return (s + o + NX) % NX

    def y_at(o):
        return (y + o + NY) % NY

    def x_dev(o):
        return {"src": x_at(o)}

    def y_dev(o):
        return {"dom": z * NY + y_at(o)}

    def z_dev(o):
        return {"dom": ((z + o + NZ) % NZ) * NY + y}

    own_copy = pltpu.make_async_copy(src, held.at[dom], own_sem)
    own_copy.start()
    val_copy = pltpu.make_async_copy(values_hbm, values, val_sem)
    val_copy.start()
    w_copy = pltpu.make_async_copy(weight_hbm, weight, w_sem)
    w_copy.start()

    near = [partner, x_dev(1), x_dev(-1), y_dev(1), y_dev(-1), y_dev(2), z_dev(1), z_dev(-1)]
    barrier = pltpu.get_barrier_semaphore()
    for to in near:
        pl.semaphore_signal(barrier, inc=1, device_id=to, device_id_type=MESH)
    own_copy.wait()
    pl.semaphore_wait(barrier, len(near))

    sent = []

    def go(copy):
        copy.start()
        sent.append(copy)
        return copy

    def send(where, row, n, s_sem, r_sem, to):
        ref = held.at[at(*where), pl.ds(row, n)]
        go(remote(ref, ref, s_sem, r_sem, to))

    def arrive(where, row, n, s_sem, r_sem):
        ref = held.at[at(*where), pl.ds(row, n)]
        remote(ref, ref, s_sem, r_sem, z_dev(1)).wait_recv()

    def cut(k, low, full, half, back):
        if k < FAR:
            return low, full
        return low + (half if back else 0), half

    def p_step(k):
        send((-(k - 1), 0), *cut(k, 0, ROWS_P, HALF_P, False), pf_s.at[k], pf_r.at[k], z_dev(1))
        send((k - 1, 0), *cut(k, 0, ROWS_P, HALF_P, True), pb_s.at[k], pb_r.at[k], z_dev(-1))

    def p_arrive(k):
        arrive((-k, 0), *cut(k, 0, ROWS_P, HALF_P, False), pf_s.at[k], pf_r.at[k])
        arrive((k, 0), *cut(k, 0, ROWS_P, HALF_P, True), pb_s.at[k], pb_r.at[k])

    def q_step(k, m):
        send((-(k - 1), m), *cut(k, ROWS_P, ROWS_Q, HALF_Q, False), qf_s.at[k, m], qf_r.at[k, m], z_dev(1))
        send((k - 1, m), *cut(k, ROWS_P, ROWS_Q, HALF_Q, True), qb_s.at[k, m], qb_r.at[k, m], z_dev(-1))

    def q_arrive(k, m):
        arrive((-k, m), *cut(k, ROWS_P, ROWS_Q, HALF_Q, False), qf_s.at[k, m], qf_r.at[k, m])
        arrive((k, m), *cut(k, ROWS_P, ROWS_Q, HALF_Q, True), qb_s.at[k, m], qb_r.at[k, m])

    def y_step(k):
        for j, zo in offsets(k):
            send((zo, 0), 0, ROWS_P, yf_s.at[j], yf_r.at[j], y_dev(1))
            send((zo, 0), 0, ROWS_P, yb_s.at[j], yb_r.at[j], y_dev(-1))

    def y_forward(k):
        for j, zo in offsets(k):
            arrive((zo, -1), 0, ROWS_P, yf_s.at[j], yf_r.at[j])
            send((zo, -1), 0, HALF_P, ff_s.at[j], ff_r.at[j], y_dev(1))
            arrive((zo, 1), 0, ROWS_P, yb_s.at[j], yb_r.at[j])
            send((zo, 1), HALF_P, HALF_P, fb_s.at[j], fb_r.at[j], y_dev(-1))

    def y_far(k):
        for j, zo in offsets(k):
            arrive((zo, 2), 0, HALF_P, ff_s.at[j], ff_r.at[j])
            arrive((zo, 2), HALF_P, HALF_P, fb_s.at[j], fb_r.at[j])

    def message(j, zo, m):
        e, before, second = tab_s[0, j], tab_s[1, j], tab_s[2, j]
        q = at(zo, m)
        block = jnp.where(second == 1, held[q, pl.ds(BLOCK, BLOCK)], held[q, pl.ds(0, BLOCK)])
        product = jnp.dot(values[e], block, preferred_element_type=F32)
        chain[j] = product + chain[before]

    def messages(k):
        for i, zo in offsets(k):
            for m in range(NY):
                message(i * NY + m, zo, m)

    p_step(1)
    send((0, 0), ROWS_P, ROWS_Q, q0_s.at[0], q0_r.at[0], y_dev(1))
    send((0, 0), ROWS_P, ROWS_Q, q0_s.at[1], q0_r.at[1], y_dev(-1))
    send((0, 0), ROWS_P, ROWS_Q, q0_s.at[2], q0_r.at[2], y_dev(2))
    q_step(1, 0)
    y_step(0)

    lanes = lax.broadcasted_iota(I32, (PARTS, PARTS), 1)
    subs = lax.broadcasted_iota(I32, (PARTS, PARTS), 0)

    def as_column(row):
        return jnp.sum(jnp.where(lanes == subs, row, 0), axis=1, keepdims=True)

    def as_row(column):
        return jnp.sum(jnp.where(lanes == subs, column, 0), axis=0, keepdims=True)

    index = subs[:, :1]
    step = index // NY
    z_off = jnp.where(step % 2 == 1, -((step + 1) // 2), step // 2)
    part = ((z + z_off + NZ) % NZ) * NY + (y + index % NY) % NY
    entry = lanes[:1, :]
    slot_of = (table[0] // 2 * REL + table[2]) * 2 + table[0] % 2
    slot_of = jnp.where(entry < count[0], slot_of, SLOTS + entry)
    reads = jnp.where(table[1] == part, 1, 0)
    entry_at = jnp.max(reads * entry, axis=1, keepdims=True)
    slot_at = jnp.max(reads * slot_of, axis=1, keepdims=True)
    pick_at = jnp.sum(jnp.where(entry == part, pick[...], 0), axis=1, keepdims=True)
    slot_row = as_row(slot_at)
    earlier = jnp.max(jnp.where((slot_row == slot_at) & (lanes < subs), lanes, -1), axis=1, keepdims=True)
    earlier = jnp.where(earlier < 0, PARTS, earlier)
    tab[...] = jnp.zeros_like(tab)
    tab[0:1, 0:PARTS] = as_row(entry_at)
    tab[1:2, 0:PARTS] = as_row(earlier)
    tab[2:3, 0:PARTS] = as_row(pick_at)
    slot_lane = lax.broadcasted_iota(I32, (PARTS, BLOCK), 1)
    order = lax.broadcasted_iota(I32, (PARTS, BLOCK), 0)
    final = jnp.max(jnp.where(slot_at == slot_lane, order, -1), axis=0, keepdims=True)
    tab[3:4, :] = jnp.where(final < 0, PARTS, final)
    chain[PARTS] = jnp.zeros((BLOCK, D), F32)

    arrive((0, -1), ROWS_P, ROWS_Q, q0_s.at[0], q0_r.at[0])
    q_step(1, 3)
    arrive((0, 1), ROWS_P, ROWS_Q, q0_s.at[1], q0_r.at[1])
    q_step(1, 1)
    arrive((0, 2), ROWS_P, ROWS_Q, q0_s.at[2], q0_r.at[2])
    q_step(1, 2)
    tab_copy = pltpu.make_async_copy(tab, tab_s, tab_sem)
    tab_copy.start()
    z_rows[...] = jnp.zeros_like(z_rows)

    events = []
    for k in range(FAR + 1):
        if k > 0:
            events.append((TIME_P[k], 0, k, "p"))
            events.append((TIME_Q[k], 2, k, "q"))
        events.append((max(TIME_Y[k], TIME_P[k] + 0.1), 1, k, "y"))
        events.append((max(TIME_Y[k] + 3.0, TIME_Q[k] + 0.1), 3, k, "m"))
    ready = False
    for _, _, k, kind in sorted(events):
        if kind == "p":
            p_arrive(k)
            if k < FAR:
                p_step(k + 1)
            y_step(k)
        elif kind == "y":
            y_forward(k)
        elif kind == "q":
            for m in (0, 3, 1, 2):
                q_arrive(k, m)
                if k < FAR:
                    q_step(k + 1, m)
        else:
            if not ready:
                val_copy.wait()
                tab_copy.wait()
                ready = True
            y_far(k)
            messages(k)

    w_copy.wait()

    def project(c, into):
        def one(r, carry):
            for h in range(2):
                last = tab_s[3, (c * REL + r) * 2 + h]
                terms[c, r, pl.ds(h * BLOCK, BLOCK)] = chain[last].astype(BF16)
            into[...] += jnp.dot(terms[c, r], weight[r], preferred_element_type=F32)
            return carry

        into[...] = jnp.zeros_like(into)
        lax.fori_loop(0, REL, one, 0)

    def blocks(body):
        def one(b, carry):
            body(pl.ds(pl.multiple_of(b * 32, 32), 32))
            return carry

        lax.fori_loop(0, 2 * BLOCK // 32, one, 0)

    panels = [x_at(2), x_at(-turn), x_at(turn), s]
    partner_panels = [x_at(2), x_at(turn), x_at(-turn), s]
    ahead, behind = x_dev(turn), x_dev(-turn)
    swaps, moves = [], []

    def combine(i):
        swaps[i].wait_recv()
        if i == 2:
            moves[0].wait_recv()

        def one(part):
            value = keep[i, part] + ex[i, part].astype(F32)
            if i == 2:
                value = value + cr[0, part].astype(F32)
            cs[i, part] = value.astype(BF16)

        blocks(one)
        moves.append(go(remote(cs.at[i], cr.at[i], cx_s.at[i], cx_r.at[i], behind if i == 1 else ahead)))

    for i in range(4):
        project(partner_panels[i] * 2 + 1 - g, work)

        def narrow(part):
            give[i, part] = work[part].astype(BF16)

        blocks(narrow)
        if i > 0:
            combine(i - 1)
        project(panels[i] * 2 + g, keep.at[i])
        swaps.append(go(remote(give.at[i], ex.at[i], ex_s.at[i], ex_r.at[i], partner)))
    swaps[3].wait_recv()
    moves[1].wait_recv()
    moves[2].wait_recv()
    own = s * 2 + g

    def activate(part):
        value = keep[3, part] + ex[3, part].astype(F32) + cr[1, part].astype(F32) + cr[2, part].astype(F32)
        logistic = 1.0 / (1.0 + jnp.exp(-value))
        result[part] = (value * logistic).astype(BF16)
        slope = logistic * (1.0 + value * (1.0 - logistic))
        rows[own, part] = (cot[part].astype(F32) * slope).astype(BF16)

    blocks(activate)

    def share(c, sem, to):
        return go(remote(rows.at[c], rows.at[c], gx_s.at[sem], gx_r.at[sem], to))

    def relay(c, sem):
        return go(remote(rows.at[c], rows.at[c], gp_s.at[sem], gp_r.at[sem], partner))

    gx0 = share(own, 0, ahead)
    gx1 = share(own, 1, behind)
    gp0 = relay(own, 0)
    out_copy = pltpu.make_async_copy(result, out, out_sem.at[0])
    out_copy.start()

    def add_terms(c, first=False):
        def one(r, carry):
            product = lax.dot_general(terms[c, r], rows[c], (((0,), (0,)), ((), ())),
                                      preferred_element_type=F32)
            if first:
                acc[r] = product
            else:
                acc[r] = acc[r] + product
            return carry

        lax.fori_loop(0, REL, one, 0)

    add_terms(own, first=True)
    gp0.wait_recv()
    add_terms(s * 2 + 1 - g)
    gx0.wait_recv()
    from_behind, from_ahead, from_far = x_at(-turn) * 2 + g, x_at(turn) * 2 + g, x_at(2) * 2 + g
    gx2 = share(from_behind, 2, ahead)
    gp1 = relay(from_behind, 1)
    gx1.wait_recv()
    gp2 = relay(from_ahead, 2)
    add_terms(from_behind)
    add_terms(from_ahead)
    gp1.wait_recv()
    add_terms(x_at(turn) * 2 + 1 - g)
    gp2.wait_recv()
    add_terms(x_at(-turn) * 2 + 1 - g)
    gx2.wait_recv()
    gp3 = relay(from_far, 3)
    add_terms(from_far)
    gp3.wait_recv()
    add_terms(x_at(2) * 2 + 1 - g)

    def ring_sum(load, stage, got, ss, rs, lane, pos, dev):
        copies = {}

        def put(k, p, to, extra):
            for r in range(3):
                value = load(r, p)
                if extra:
                    value = value + got[0, r].astype(F32)
                stage[k, r] = value.astype(BF16)
            copies[k] = go(remote(stage.at[k], got.at[k], ss.at[lane, k], rs.at[lane, k], to))

        def begin():
            put(0, pos(2), dev(turn), False)
            put(1, pos(-turn), dev(-turn), False)

        def middle():
            copies[0].wait_recv()
            put(2, pos(turn), dev(turn), True)

        def end(store):
            copies[1].wait_recv()
            copies[2].wait_recv()
            for r in range(3):
                store(r, load(r, pos(0)) + got[1, r].astype(F32) + got[2, r].astype(F32))

        return begin, middle, end

    def both(one, two, *ends):
        one[0]()
        two[0]()
        one[1]()
        two[1]()
        one[2](*ends[:1])
        two[2](*ends[1:])

    def into_a(r, value):
        a_sum[r] = value

    def into_b(r, value):
        b_sum[r] = value

    def into_tail_a(r, value):
        tail[r] = value

    def into_tail_b(r, value):
        tail[3 + r] = value

    both(ring_sum(lambda r, p: acc[r, pl.ds(p * 64, 64)], a_send, a_recv, s1_s, s1_r, 0, x_at, x_dev),
         ring_sum(lambda r, p: acc[3 + r, pl.ds(p * 64, 64)], b_send, b_recv, s1_s, s1_r, 1, y_at, y_dev),
         into_a, into_b)
    both(ring_sum(lambda r, p: a_sum[r, pl.ds(p * 16, 16)], a2_send, a2_recv, s2_s, s2_r, 0, y_at, y_dev),
         ring_sum(lambda r, p: b_sum[r, pl.ds(p * 16, 16)], b2_send, b2_recv, s2_s, s2_r, 1, x_at, x_dev),
         into_tail_a, into_tail_b)
    for j in range(NZ):
        for r in range(REL):
            for h in range(2):
                z_rows[j, pl.ds(2 * r + h, 1)] = tail[r, pl.ds(j, 1), pl.ds(h * BLOCK, BLOCK)]
    z_send[...] = z_rows[...].astype(BF16)
    third = []
    for d in range(1, NZ):
        to = (z + d) % NZ
        third.append(go(remote(z_send.at[to], z_recv.at[d], z1_s.at[d], z1_r.at[d], z_dev(d))))
    value = z_rows[z]
    for d in range(1, NZ):
        third[d - 1].wait_recv()
        value = value + z_recv[d].astype(F32)
    z_full[z] = value.astype(BF16)

    fourth = []
    for d in range(1, NZ):
        fourth.append(go(remote(z_full.at[z], z_full.at[z], z2_s.at[d], z2_r.at[d], z_dev(d))))
    for copy in fourth:
        copy.wait_recv()
    z_rows[...] = z_full[...].astype(F32)
    for j in range(NZ):
        for r in range(REL):
            for h in range(2):
                tail[r, pl.ds(j, 1), pl.ds(h * BLOCK, BLOCK)] = z_rows[j, pl.ds(2 * r + h, 1)]
    for r in range(3):
        a_all[s, y, r] = tail[r].astype(BF16)
        b_all[y, s, r] = tail[3 + r].astype(BF16)

    def ring_spread(ref, ss, rs, lane, pos, dev):
        copies = {}

        def put(k, p, to):
            copies[k] = go(remote(ref(p), ref(p), ss.at[lane, k], rs.at[lane, k], to))

        def begin():
            put(0, pos(0), dev(turn))
            put(1, pos(0), dev(-turn))

        def middle():
            copies[0].wait_recv()
            put(2, pos(-turn), dev(turn))

        def end():
            copies[1].wait_recv()
            copies[2].wait_recv()

        return begin, middle, end

    both(ring_spread(lambda p: a_all.at[s, p], s4_s, s4_r, 0, y_at, y_dev),
         ring_spread(lambda p: b_all.at[y, p], s4_s, s4_r, 1, x_at, x_dev))
    both(ring_spread(lambda p: a_all.at[p], s5_s, s5_r, 0, x_at, x_dev),
         ring_spread(lambda p: b_all.at[p], s5_s, s5_r, 1, y_at, y_dev))
    a_copy = pltpu.make_async_copy(a_all, a_out, out_sem.at[1])
    b_copy = pltpu.make_async_copy(b_all, b_out, out_sem.at[2])
    a_copy.start()
    b_copy.start()
    for copy in sent:
        copy.wait_send()
    out_copy.wait()
    a_copy.wait()
    b_copy.wait()


def layer(source_feats, table, pick, count, values, weight, cotangent):
    hbm = pl.BlockSpec(memory_space=pl.ANY)
    vmem = pl.BlockSpec(memory_space=pltpu.VMEM)
    smem = pl.BlockSpec(memory_space=pltpu.SMEM)
    dma = pltpu.SemaphoreType.DMA
    V = pltpu.VMEM
    steps = FAR + 1
    slots = values.shape[0]
    sums = jax.ShapeDtypeStruct((4, 4, 3, 16, D), BF16)
    return pl.pallas_call(
        layer_kernel,
        out_shape=(jax.ShapeDtypeStruct((2 * BLOCK, D), BF16), sums, sums),
        in_specs=[hbm, vmem, vmem, smem, hbm, hbm, vmem],
        out_specs=(hbm, hbm, hbm),
        scratch_shapes=[
            V((PARTS, 2 * BLOCK, D), BF16), V((slots, BLOCK, BLOCK), BF16), V((REL, D, D), BF16),
            V((PARTS + 1, BLOCK, D), F32), V((8, BLOCK), I32), pltpu.SMEM((8, BLOCK), I32),
            V((CHUNKS, REL, 256, D), BF16), V((256, D), F32), V((4, 256, D), F32), V((4, 256, D), BF16),
            V((4, 256, D), BF16), V((3, 256, D), BF16), V((3, 256, D), BF16), V((CHUNKS, 256, D), BF16),
            V((REL, D, D), F32),
            V((256, D), BF16), V((4, 4, 3, 16, D), BF16), V((4, 4, 3, 16, D), BF16),
            V((3, 3, 64, D), BF16), V((3, 3, 64, D), BF16), V((3, 3, 64, D), BF16), V((3, 3, 64, D), BF16),
            V((3, 64, D), F32), V((3, 64, D), F32),
            V((3, 3, 16, D), BF16), V((3, 3, 16, D), BF16), V((3, 3, 16, D), BF16), V((3, 3, 16, D), BF16),
            V((REL, 16, D), F32), V((NZ, 16, BLOCK), F32), V((NZ, 16, BLOCK), BF16),
            V((NZ, 16, BLOCK), BF16), V((NZ, 16, BLOCK), BF16),
            dma, dma, dma, dma, dma((3,))]
        + [dma((steps,))] * 4 + [dma((NZ,))] * 8 + [dma((3,))] * 2 + [dma((steps, NY))] * 4
        + [dma((4,))] * 2 + [dma((3,))] * 2 + [dma((3,))] * 2 + [dma((4,))] * 2
        + [dma((2, 3))] * 4 + [dma((NZ,))] * 4 + [dma((2, 3))] * 4,
        compiler_params=pltpu.CompilerParams(
            collective_id=0, has_side_effects=True, vmem_limit_bytes=60 << 20),
        name="layer",
    )(source_feats, table, pick, count, values, weight, cotangent)


def finish_kernel(result, a_all, b_all, out, grad):
    out[...] = result[...]
    for i in range(4):
        for j in range(4):
            part = pl.ds(64 * i + 16 * j, 16)
            for r in range(3):
                grad[r, part] = a_all[i, j, r].astype(F32)
                grad[3 + r, part] = b_all[i, j, r].astype(F32)


def finish(result, a_all, b_all):
    vmem = pl.BlockSpec(memory_space=pltpu.VMEM)
    return pl.pallas_call(
        finish_kernel,
        out_shape=(jax.ShapeDtypeStruct((2 * BLOCK, D), BF16),
                   jax.ShapeDtypeStruct((REL, D, D), F32)),
        in_specs=[vmem] * 3,
        out_specs=(vmem, vmem),
        name="finish",
    )(result, a_all, b_all)


def local(source_feats, rel_weight, halo_pick, entry_index, entry_count, entry_values, cotangent):
    slots = entry_index.shape[-1]
    return finish(*layer(
        source_feats, entry_index.reshape(3, 1, slots), halo_pick.reshape(1, -1), entry_count.reshape(1),
        entry_values.reshape(slots, BLOCK, BLOCK), rel_weight, cotangent))


def solution(mesh):
    return jax.shard_map(
        local,
        mesh=mesh,
        in_specs=(
            P(("dom", "src", "rel"), None),
            P("rel", None, None),
            P("dom", "src", "rel", None),
            P("dom", "src", "rel", None, None),
            P("dom", "src", "rel"),
            P("dom", "src", "rel", None, None, None),
            P(("dom", "src", "rel"), None),
        ),
        out_specs=(P(("dom", "src", "rel"), None), P("rel", None, None)),
        check_vma=False,
    )
```

time: 712 us -> 148 us (0.21)
  waiting for transfers between devices: 639 us -> 0 us
  Pallas kernels: 0 us -> 147 us
  local copies, waits for them, and re-layouts: 29.3 us -> 0 us
  matrix products: 24.4 us -> 0 us
  between operations: 14.5 us -> 1.29 us
    psum x1 -> x0, waiting for transfers between devices: 412 us -> none  [local(): grad_rel = lax.psum(weight_terms, ('dom', 'src'))]
    all_gather x2 -> x0, waiting for transfers between devices: 193 us -> none  [the longest x1 161 us: local(): everyone = lax.all_gather(source_feats, 'dom', axis=0, tiled=True)]
    pallas_call x0 -> x2, Pallas kernels: none -> 147 us  [the longest x1 144 us: layer(): pl.pallas_call(layer_kernel, out_shape=(jax.ShapeDtypeStruct((2 * BLOCK,...]
    reduce_scatter x1 -> x0, waiting for transfers between devices: 33.4 us -> none  [local(): lax.psum_scatter(jnp.einsum('rtd,rde->te', relation_terms, rel_weight, pr...]
    dot_general x4 -> x0, matrix products: 24.4 us -> none  [the longest x1 8.45 us: local(): jnp.einsum('se,eid->sid', placement, messages, precision=lax.Precision.HI...]
    gather x2 -> x0, local copies, waits for them, and re-layouts: 11.1 us -> none  [the longest x1 6.16 us: local(): halo_blocks = everyone[jnp.arange(partitions, dtype=jnp.int32), chosen]]
    dot_general x1 -> x0, local copies, waits for them, and re-layouts: 9.16 us -> none  [local(): jnp.einsum('eij,ejd->eid', values, picked, preferred_element_type=jnp.flo...]
  transfers between devices with their start and end apart: 4 -> 0, of which waited for: 4 -> 0; matrix products, arithmetic and copies ran while one was open for 0% -> 0% of each run, Pallas kernels for 0% -> 0%
where the time goes in v2:
time: 148 us
  Pallas kernels  147 us (99%)
    pallas_call x1, Pallas kernels, layer(): pl.pallas_call(layer_kernel, out_shape=(jax.ShapeDtypeStruct((2 * BLOCK,...  144 us

profile of v2, /device:TPU:2, one launch (start us, length us, event | category | flops | bytes accessed | tf_op | source)
XLA Modules:
  0.0 147.9 jit_solution(17122706138073139153)
XLA Ops:
  1.3 144.2 %layer.1 = (bf16[256,256]{1,0:T(8,128)(2,1)}, bf16[4,4,3,16,256]{4,3,2,1,0:T(8,128)(2,1)}, bf16[4,4,3,16,256]{4,3,2,1,0:T(8,128)(2,1)}) custom-call(bf16[256,256]{1,0:T(8,128)(2,1)} %src.1, s32[3,1,64]{2,1,0:T(1,128)} %bitcast.6, s32[1,64]{1,0:T(1,128)} %bitcast.7, s32[1]{0:T(128)} %bitcast.4.count, bf16[64,128,128]{2,1,0:T(8,128)(2,1)} %bitcast.5, ...), custom_call_target="tpu_custom_call" | custom-call | tf_op jit(solution)/shard_map/layer/pallas_call | solution.py:474
  145.4 2.4 %finish.1 = (bf16[256,256]{1,0:T(8,128)(2,1)}, f32[6,256,256]{2,1,0:T(8,128)}) custom-call(bf16[256,256]{1,0:T(8,128)(2,1)} %get-tuple-element.5.result, bf16[4,4,3,16,256]{4,3,2,1,0:T(8,128)(2,1)} %get-tuple-element.6.a_all, bf16[4,4,3,16,256]{4,3,2,1,0:T(8,128)(2,1)} %get-tuple-element.7.b_all), custom_call_target="tpu_custom_call" | custom-call | tf_op jit(solution)/shard_map/finish/pallas_call | solution.py:513

commit v3 on v2

--- a/solution.py
+++ b/solution.py
@@ -19,21 +19,26 @@
 REL = 6
 CHUNKS = 8
 SLOTS = CHUNKS * REL * 2
-ROWS_P = 160
-HALF_P = 80
-ROWS_Q = 96
-HALF_Q = 48
+ROWS_P = 96
+HALF_P = 48
+ROWS_Q = 32
+HALF_Q = 16
 FAR = NZ // 2
 
-TIME_P = [0.0] + [4.0 * k for k in range(1, 9)]
-TIME_Y = [3.0, 8.0, 13.2, 18.5, 24.0, 29.0, 34.5, 39.7, 44.0]
-TIME_Q = [0.0, 7.5, 15.0, 22.5, 30.0, 35.0, 39.0, 43.0, 45.0]
+TIME_P = [5.0 * k for k in range(FAR + 1)]
+TIME_Q = [5.0 * k + 1.0 for k in range(FAR + 1)]
+TIME_Y = [5.0 * k + 6.0 for k in range(FAR + 1)]
+MESSAGE_LAG = 8.5
 
 
 def remote(src, dst, send_sem, recv_sem, to):
     return pltpu.make_async_remote_copy(
         src_ref=src, dst_ref=dst, send_sem=send_sem, recv_sem=recv_sem,
         device_id=to, device_id_type=MESH)
+
+
+def choose(second, one, zero):
+    return jnp.where(second == 1, one, zero)
 
 
 def offsets(k):
@@ -46,11 +51,12 @@
 
 def layer_kernel(src, table, pick, count, values_hbm, weight_hbm, cot,
                  out, a_out, b_out,
-                 held, values, weight, chain, tab, tab_s, terms, work, keep, give, ex, cs, cr, rows, acc,
+                 held, got, stage_up, stage_down, stage_far, relay_up, relay_down, my_pick, peer_pick, peer_s,
+                 values, weight, chain, tab, tab_s, terms, work, keep, give, ex, cs, cr, rows, acc,
                  result, a_all, b_all,
                  a_send, a_recv, b_send, b_recv, a_sum, b_sum,
                  a2_send, a2_recv, b2_send, b2_recv, tail, z_rows, z_send, z_recv, z_full,
-                 own_sem, val_sem, w_sem, tab_sem, out_sem,
+                 own_sem, val_sem, w_sem, tab_sem, out_sem, pick_sem, pp_s, pp_r, hu_s, hu_r, hd_s, hd_r,
                  pf_s, pf_r, pb_s, pb_r, yf_s, yf_r, yb_s, yb_r,
                  ff_s, ff_r, fb_s, fb_r, q0_s, q0_r, qf_s, qf_r, qb_s, qb_r,
                  ex_s, ex_r, cx_s, cx_r, gx_s, gx_r, gp_s, gp_r,
@@ -89,6 +95,8 @@
     barrier = pltpu.get_barrier_semaphore()
     for to in near:
         pl.semaphore_signal(barrier, inc=1, device_id=to, device_id_type=MESH)
+    my_pick[...] = jnp.zeros_like(my_pick)
+    my_pick[0:1, 0:PARTS] = pick[...]
     own_copy.wait()
     pl.semaphore_wait(barrier, len(near))
 
@@ -100,11 +108,11 @@
         return copy
 
     def send(where, row, n, s_sem, r_sem, to):
-        ref = held.at[at(*where), pl.ds(row, n)]
+        ref = held.at[at(*where), :, pl.ds(row, n)]
         go(remote(ref, ref, s_sem, r_sem, to))
 
     def arrive(where, row, n, s_sem, r_sem):
-        ref = held.at[at(*where), pl.ds(row, n)]
+        ref = held.at[at(*where), :, pl.ds(row, n)]
         remote(ref, ref, s_sem, r_sem, z_dev(1)).wait_recv()
 
     def cut(k, low, full, half, back):
@@ -130,38 +138,66 @@
 
     def y_step(k):
         for j, zo in offsets(k):
-            send((zo, 0), 0, ROWS_P, yf_s.at[j], yf_r.at[j], y_dev(1))
-            send((zo, 0), 0, ROWS_P, yb_s.at[j], yb_r.at[j], y_dev(-1))
+            q = at(zo, 0)
+            top = pl.ds(0, ROWS_P)
+            stage_far[j] = choose(peer_s[2, 0, q], held[q, 1, top], held[q, 0, top])
+            stage_up[j] = choose(peer_s[0, 0, q], held[q, 1, top], held[q, 0, top])
+            stage_down[j] = choose(peer_s[1, 0, q], held[q, 1, top], held[q, 0, top])
+            go(remote(stage_far.at[j, pl.ds(0, HALF_P)], relay_up.at[j], hu_s.at[j], hu_r.at[j], y_dev(1)))
+            go(remote(stage_far.at[j, pl.ds(HALF_P, HALF_P)], relay_down.at[j], hd_s.at[j], hd_r.at[j], y_dev(-1)))
+            go(remote(stage_up.at[j], got.at[j, 3, top], yf_s.at[j], yf_r.at[j], y_dev(1)))
+            go(remote(stage_down.at[j], got.at[j, 1, top], yb_s.at[j], yb_r.at[j], y_dev(-1)))
+
+    def landed(ref, s_sem, r_sem):
+        remote(ref, ref, s_sem, r_sem, y_dev(1)).wait_recv()
 
     def y_forward(k):
         for j, zo in offsets(k):
-            arrive((zo, -1), 0, ROWS_P, yf_s.at[j], yf_r.at[j])
-            send((zo, -1), 0, HALF_P, ff_s.at[j], ff_r.at[j], y_dev(1))
-            arrive((zo, 1), 0, ROWS_P, yb_s.at[j], yb_r.at[j])
-            send((zo, 1), HALF_P, HALF_P, fb_s.at[j], fb_r.at[j], y_dev(-1))
+            landed(relay_up.at[j], hu_s.at[j], hu_r.at[j])
+            go(remote(relay_up.at[j], got.at[j, 2, pl.ds(0, HALF_P)], ff_s.at[j], ff_r.at[j], y_dev(1)))
+            landed(relay_down.at[j], hd_s.at[j], hd_r.at[j])
+            go(remote(relay_down.at[j], got.at[j, 2, pl.ds(HALF_P, HALF_P)], fb_s.at[j], fb_r.at[j], y_dev(-1)))
 
     def y_far(k):
         for j, zo in offsets(k):
-            arrive((zo, 2), 0, HALF_P, ff_s.at[j], ff_r.at[j])
-            arrive((zo, 2), HALF_P, HALF_P, fb_s.at[j], fb_r.at[j])
-
-    def message(j, zo, m):
+            landed(got.at[j, 3, pl.ds(0, ROWS_P)], yf_s.at[j], yf_r.at[j])
+            landed(got.at[j, 1, pl.ds(0, ROWS_P)], yb_s.at[j], yb_r.at[j])
+            landed(got.at[j, 2, pl.ds(0, HALF_P)], ff_s.at[j], ff_r.at[j])
+            landed(got.at[j, 2, pl.ds(HALF_P, HALF_P)], fb_s.at[j], fb_r.at[j])
+
+    def message(i, zo, m):
+        j = i * NY + m
         e, before, second = tab_s[0, j], tab_s[1, j], tab_s[2, j]
         q = at(zo, m)
-        block = jnp.where(second == 1, held[q, pl.ds(BLOCK, BLOCK)], held[q, pl.ds(0, BLOCK)])
+        if m == 0:
+            block = choose(second, held[q, 1], held[q, 0])
+        else:
+            rest = pl.ds(ROWS_P, ROWS_Q)
+            block = jnp.concatenate(
+                [got[i, m, pl.ds(0, ROWS_P)], choose(second, held[q, 1, rest], held[q, 0, rest])], axis=0)
         product = jnp.dot(values[e], block, preferred_element_type=F32)
         chain[j] = product + chain[before]
 
     def messages(k):
         for i, zo in offsets(k):
             for m in range(NY):
-                message(i * NY + m, zo, m)
+                message(i, zo, m)
 
     p_step(1)
+    swaps_of_picks = []
+    for i, o in enumerate((1, -1, 2)):
+        there = (1, 0, 2)[i]
+        swaps_of_picks.append(go(remote(my_pick, peer_pick.at[there], pp_s.at[i], pp_r.at[there], y_dev(o))))
     send((0, 0), ROWS_P, ROWS_Q, q0_s.at[0], q0_r.at[0], y_dev(1))
     send((0, 0), ROWS_P, ROWS_Q, q0_s.at[1], q0_r.at[1], y_dev(-1))
     send((0, 0), ROWS_P, ROWS_Q, q0_s.at[2], q0_r.at[2], y_dev(2))
     q_step(1, 0)
+
+    for i in range(3):
+        landed(peer_pick.at[i], pp_s.at[i], pp_r.at[i])
+    pick_copy = pltpu.make_async_copy(peer_pick, peer_s, pick_sem)
+    pick_copy.start()
+    pick_copy.wait()
     y_step(0)
 
     lanes = lax.broadcasted_iota(I32, (PARTS, PARTS), 1)
@@ -213,7 +249,7 @@
             events.append((TIME_P[k], 0, k, "p"))
             events.append((TIME_Q[k], 2, k, "q"))
         events.append((max(TIME_Y[k], TIME_P[k] + 0.1), 1, k, "y"))
-        events.append((max(TIME_Y[k] + 3.0, TIME_Q[k] + 0.1), 3, k, "m"))
+        events.append((max(TIME_Y[k] + MESSAGE_LAG, TIME_Q[k] + 0.1), 3, k, "m"))
     ready = False
     for _, _, k, kind in sorted(events):
         if kind == "p":
@@ -477,7 +513,11 @@
         in_specs=[hbm, vmem, vmem, smem, hbm, hbm, vmem],
         out_specs=(hbm, hbm, hbm),
         scratch_shapes=[
-            V((PARTS, 2 * BLOCK, D), BF16), V((slots, BLOCK, BLOCK), BF16), V((REL, D, D), BF16),
+            V((PARTS, 2, BLOCK, D), BF16), V((NZ, NY, BLOCK, D), BF16),
+            V((NZ, ROWS_P, D), BF16), V((NZ, ROWS_P, D), BF16), V((NZ, ROWS_P, D), BF16),
+            V((NZ, HALF_P, D), BF16), V((NZ, HALF_P, D), BF16),
+            V((8, BLOCK), I32), V((3, 8, BLOCK), I32), pltpu.SMEM((3, 8, BLOCK), I32),
+            V((slots, BLOCK, BLOCK), BF16), V((REL, D, D), BF16),
             V((PARTS + 1, BLOCK, D), F32), V((8, BLOCK), I32), pltpu.SMEM((8, BLOCK), I32),
             V((CHUNKS, REL, 256, D), BF16), V((256, D), F32), V((4, 256, D), F32), V((4, 256, D), BF16),
             V((4, 256, D), BF16), V((3, 256, D), BF16), V((3, 256, D), BF16), V((CHUNKS, 256, D), BF16),
@@ -488,7 +528,8 @@
             V((3, 3, 16, D), BF16), V((3, 3, 16, D), BF16), V((3, 3, 16, D), BF16), V((3, 3, 16, D), BF16),
             V((REL, 16, D), F32), V((NZ, 16, BLOCK), F32), V((NZ, 16, BLOCK), BF16),
             V((NZ, 16, BLOCK), BF16), V((NZ, 16, BLOCK), BF16),
-            dma, dma, dma, dma, dma((3,))]
+            dma, dma, dma, dma, dma((3,)), dma, dma((3,)), dma((3,))]
+        + [dma((NZ,))] * 4
         + [dma((steps,))] * 4 + [dma((NZ,))] * 8 + [dma((3,))] * 2 + [dma((steps, NY))] * 4
         + [dma((4,))] * 2 + [dma((3,))] * 2 + [dma((3,))] * 2 + [dma((4,))] * 2
         + [dma((2, 3))] * 4 + [dma((NZ,))] * 4 + [dma((2, 3))] * 4,
@@ -523,7 +564,7 @@
 def local(source_feats, rel_weight, halo_pick, entry_index, entry_count, entry_values, cotangent):
     slots = entry_index.shape[-1]
     return finish(*layer(
-        source_feats, entry_index.reshape(3, 1, slots), halo_pick.reshape(1, -1), entry_count.reshape(1),
+        source_feats.reshape(2, BLOCK, D), entry_index.reshape(3, 1, slots), halo_pick.reshape(1, -1), entry_count.reshape(1),
         entry_values.reshape(slots, BLOCK, BLOCK), rel_weight, cotangent))
 
 

time: 148 us -> 139 us (0.939)
  Pallas kernels: 147 us -> 137 us
    pallas_call x1, Pallas kernels: 144 us -> 135 us  [layer(): pl.pallas_call(layer_kernel, out_shape=(jax.ShapeDtypeStruct((2 * BLOCK,...]
where the time goes in v3:
time: 139 us
  Pallas kernels  137 us (99%)
    pallas_call x1, Pallas kernels, layer(): pl.pallas_call(layer_kernel, out_shape=(jax.ShapeDtypeStruct((2 * BLOCK,...  135 us

profile of v3, /device:TPU:2, one launch (start us, length us, event | category | flops | bytes accessed | tf_op | source)
XLA Modules:
  0.0 138.7 jit_solution(17831972783506922554)
XLA Ops:
  1.3 135.0 %layer.1 = (bf16[256,256]{1,0:T(8,128)(2,1)}, bf16[4,4,3,16,256]{4,3,2,1,0:T(8,128)(2,1)}, bf16[4,4,3,16,256]{4,3,2,1,0:T(8,128)(2,1)}) custom-call(bf16[2,128,256]{2,1,0:T(8,128)(2,1)} %bitcast.7, s32[3,1,64]{2,1,0:T(1,128)} %bitcast.8, s32[1,64]{1,0:T(1,128)} %bitcast.9, s32[1]{0:T(128)} %bitcast.5.count, bf16[64,128,128]{2,1,0:T(8,128)(2,1)} %bitcast.6, ...), custom_call_target="tpu_custom_call" | custom-call | tf_op jit(solution)/shard_map/layer/pallas_call | solution.py:510
  136.2 2.4 %finish.1 = (bf16[256,256]{1,0:T(8,128)(2,1)}, f32[6,256,256]{2,1,0:T(8,128)}) custom-call(bf16[256,256]{1,0:T(8,128)(2,1)} %get-tuple-element.5.result, bf16[4,4,3,16,256]{4,3,2,1,0:T(8,128)(2,1)} %get-tuple-element.6.a_all, bf16[4,4,3,16,256]{4,3,2,1,0:T(8,128)(2,1)} %get-tuple-element.7.b_all), custom_call_target="tpu_custom_call" | custom-call | tf_op jit(solution)/shard_map/finish/pallas_call | solution.py:554

commit v4 on v3

--- a/solution.py
+++ b/solution.py
@@ -285,12 +285,14 @@
         into[...] = jnp.zeros_like(into)
         lax.fori_loop(0, REL, one, 0)
 
-    def blocks(body):
+    def blocks(body, low, n):
         def one(b, carry):
-            body(pl.ds(pl.multiple_of(b * 32, 32), 32))
+            body(pl.ds(pl.multiple_of(low + b * 32, 32), 32))
             return carry
 
-        lax.fori_loop(0, 2 * BLOCK // 32, one, 0)
+        lax.fori_loop(0, n // 32, one, 0)
+
+    halves = [pl.ds(h * BLOCK, BLOCK) for h in range(2)]
 
     panels = [x_at(2), x_at(-turn), x_at(turn), s]
     partner_panels = [x_at(2), x_at(turn), x_at(-turn), s]
@@ -299,17 +301,21 @@
 
     def combine(i):
         swaps[i].wait_recv()
-        if i == 2:
-            moves[0].wait_recv()
-
-        def one(part):
-            value = keep[i, part] + ex[i, part].astype(F32)
+        copies = []
+        for h in range(2):
             if i == 2:
-                value = value + cr[0, part].astype(F32)
-            cs[i, part] = value.astype(BF16)
-
-        blocks(one)
-        moves.append(go(remote(cs.at[i], cr.at[i], cx_s.at[i], cx_r.at[i], behind if i == 1 else ahead)))
+                moves[0][h].wait_recv()
+
+            def one(part):
+                value = keep[i, part] + ex[i, part].astype(F32)
+                if i == 2:
+                    value = value + cr[0, part].astype(F32)
+                cs[i, part] = value.astype(BF16)
+
+            blocks(one, h * BLOCK, BLOCK)
+            copies.append(go(remote(cs.at[i, halves[h]], cr.at[i, halves[h]], cx_s.at[i, h], cx_r.at[i, h],
+                                    behind if i == 1 else ahead)))
+        moves.append(copies)
 
     for i in range(4):
         project(partner_panels[i] * 2 + 1 - g, work)
@@ -317,14 +323,12 @@
         def narrow(part):
             give[i, part] = work[part].astype(BF16)
 
-        blocks(narrow)
+        blocks(narrow, 0, 2 * BLOCK)
         if i > 0:
             combine(i - 1)
         project(panels[i] * 2 + g, keep.at[i])
         swaps.append(go(remote(give.at[i], ex.at[i], ex_s.at[i], ex_r.at[i], partner)))
     swaps[3].wait_recv()
-    moves[1].wait_recv()
-    moves[2].wait_recv()
     own = s * 2 + g
 
     def activate(part):
@@ -334,17 +338,27 @@
         slope = logistic * (1.0 + value * (1.0 - logistic))
         rows[own, part] = (cot[part].astype(F32) * slope).astype(BF16)
 
-    blocks(activate)
-
-    def share(c, sem, to):
-        return go(remote(rows.at[c], rows.at[c], gx_s.at[sem], gx_r.at[sem], to))
-
-    def relay(c, sem):
-        return go(remote(rows.at[c], rows.at[c], gp_s.at[sem], gp_r.at[sem], partner))
-
-    gx0 = share(own, 0, ahead)
-    gx1 = share(own, 1, behind)
-    gp0 = relay(own, 0)
+    def share(c, sem, to, h):
+        ref = rows.at[c, halves[h]]
+        return go(remote(ref, ref, gx_s.at[sem, h], gx_r.at[sem, h], to))
+
+    def relay(c, sem, h):
+        ref = rows.at[c, halves[h]]
+        return go(remote(ref, ref, gp_s.at[sem, h], gp_r.at[sem, h], partner))
+
+    gx0, gx1, gx2, gp0, gp1, gp2, gp3 = [], [], [], [], [], [], []
+    for h in range(2):
+        moves[1][h].wait_recv()
+        moves[2][h].wait_recv()
+        blocks(activate, h * BLOCK, BLOCK)
+        gx0.append(share(own, 0, ahead, h))
+        gx1.append(share(own, 1, behind, h))
+        gp0.append(relay(own, 0, h))
+
+    def wait_both(copies):
+        for copy in copies:
+            copy.wait_recv()
+
     out_copy = pltpu.make_async_copy(result, out, out_sem.at[0])
     out_copy.start()
 
@@ -361,60 +375,58 @@
         lax.fori_loop(0, REL, one, 0)
 
     add_terms(own, first=True)
-    gp0.wait_recv()
+    wait_both(gp0)
     add_terms(s * 2 + 1 - g)
-    gx0.wait_recv()
     from_behind, from_ahead, from_far = x_at(-turn) * 2 + g, x_at(turn) * 2 + g, x_at(2) * 2 + g
-    gx2 = share(from_behind, 2, ahead)
-    gp1 = relay(from_behind, 1)
-    gx1.wait_recv()
-    gp2 = relay(from_ahead, 2)
+    for h in range(2):
+        gx0[h].wait_recv()
+        gx2.append(share(from_behind, 2, ahead, h))
+        gp1.append(relay(from_behind, 1, h))
+    for h in range(2):
+        gx1[h].wait_recv()
+        gp2.append(relay(from_ahead, 2, h))
     add_terms(from_behind)
     add_terms(from_ahead)
-    gp1.wait_recv()
+    wait_both(gp1)
     add_terms(x_at(turn) * 2 + 1 - g)
-    gp2.wait_recv()
+    wait_both(gp2)
     add_terms(x_at(-turn) * 2 + 1 - g)
-    gx2.wait_recv()
-    gp3 = relay(from_far, 3)
+    for h in range(2):
+        gx2[h].wait_recv()
+        gp3.append(relay(from_far, 3, h))
     add_terms(from_far)
-    gp3.wait_recv()
+    wait_both(gp3)
     add_terms(x_at(2) * 2 + 1 - g)
 
     def ring_sum(load, stage, got, ss, rs, lane, pos, dev):
         copies = {}
 
-        def put(k, p, to, extra):
-            for r in range(3):
-                value = load(r, p)
-                if extra:
-                    value = value + got[0, r].astype(F32)
-                stage[k, r] = value.astype(BF16)
-            copies[k] = go(remote(stage.at[k], got.at[k], ss.at[lane, k], rs.at[lane, k], to))
-
-        def begin():
-            put(0, pos(2), dev(turn), False)
-            put(1, pos(-turn), dev(-turn), False)
-
-        def middle():
-            copies[0].wait_recv()
-            put(2, pos(turn), dev(turn), True)
-
-        def end(store):
-            copies[1].wait_recv()
-            copies[2].wait_recv()
-            for r in range(3):
-                store(r, load(r, pos(0)) + got[1, r].astype(F32) + got[2, r].astype(F32))
-
-        return begin, middle, end
-
-    def both(one, two, *ends):
-        one[0]()
-        two[0]()
-        one[1]()
-        two[1]()
-        one[2](*ends[:1])
-        two[2](*ends[1:])
+        def put(k, p, to, r):
+            value = load(r, p)
+            if k == 2:
+                copies[0, r].wait_recv()
+                value = value + got[0, r].astype(F32)
+            stage[k, r] = value.astype(BF16)
+            copies[k, r] = go(remote(stage.at[k, r], got.at[k, r], ss.at[lane, k, r], rs.at[lane, k, r], to))
+
+        def end(r):
+            copies[1, r].wait_recv()
+            copies[2, r].wait_recv()
+            return load(r, pos(0)) + got[1, r].astype(F32) + got[2, r].astype(F32)
+
+        return (lambda r: put(0, pos(2), dev(turn), r), lambda r: put(1, pos(-turn), dev(-turn), r),
+                lambda r: put(2, pos(turn), dev(turn), r), end)
+
+    def both(one, two, n, store=None):
+        for phase in range(3):
+            for r in range(n):
+                one[phase](r)
+                two[phase](r)
+        for r in range(n):
+            value_a, value_b = one[3](r), two[3](r)
+            if store is not None:
+                store[0](r, value_a)
+                store[1](r, value_b)
 
     def into_a(r, value):
         a_sum[r] = value
@@ -430,10 +442,10 @@
 
     both(ring_sum(lambda r, p: acc[r, pl.ds(p * 64, 64)], a_send, a_recv, s1_s, s1_r, 0, x_at, x_dev),
          ring_sum(lambda r, p: acc[3 + r, pl.ds(p * 64, 64)], b_send, b_recv, s1_s, s1_r, 1, y_at, y_dev),
-         into_a, into_b)
+         3, (into_a, into_b))
     both(ring_sum(lambda r, p: a_sum[r, pl.ds(p * 16, 16)], a2_send, a2_recv, s2_s, s2_r, 0, y_at, y_dev),
          ring_sum(lambda r, p: b_sum[r, pl.ds(p * 16, 16)], b2_send, b2_recv, s2_s, s2_r, 1, x_at, x_dev),
-         into_tail_a, into_tail_b)
+         3, (into_tail_a, into_tail_b))
     for j in range(NZ):
         for r in range(REL):
             for h in range(2):
@@ -466,27 +478,22 @@
     def ring_spread(ref, ss, rs, lane, pos, dev):
         copies = {}
 
-        def put(k, p, to):
-            copies[k] = go(remote(ref(p), ref(p), ss.at[lane, k], rs.at[lane, k], to))
-
-        def begin():
-            put(0, pos(0), dev(turn))
-            put(1, pos(0), dev(-turn))
-
-        def middle():
-            copies[0].wait_recv()
-            put(2, pos(-turn), dev(turn))
-
-        def end():
-            copies[1].wait_recv()
-            copies[2].wait_recv()
-
-        return begin, middle, end
-
-    both(ring_spread(lambda p: a_all.at[s, p], s4_s, s4_r, 0, y_at, y_dev),
-         ring_spread(lambda p: b_all.at[y, p], s4_s, s4_r, 1, x_at, x_dev))
-    both(ring_spread(lambda p: a_all.at[p], s5_s, s5_r, 0, x_at, x_dev),
-         ring_spread(lambda p: b_all.at[p], s5_s, s5_r, 1, y_at, y_dev))
+        def put(k, p, to, t):
+            if k == 2:
+                copies[0, t].wait_recv()
+            copies[k, t] = go(remote(ref(p, t), ref(p, t), ss.at[lane, k, t], rs.at[lane, k, t], to))
+
+        def end(t):
+            copies[1, t].wait_recv()
+            copies[2, t].wait_recv()
+
+        return (lambda t: put(0, pos(0), dev(turn), t), lambda t: put(1, pos(0), dev(-turn), t),
+                lambda t: put(2, pos(-turn), dev(turn), t), end)
+
+    both(ring_spread(lambda p, t: a_all.at[s, p], s4_s, s4_r, 0, y_at, y_dev),
+         ring_spread(lambda p, t: b_all.at[y, p], s4_s, s4_r, 1, x_at, x_dev), 1)
+    both(ring_spread(lambda p, t: a_all.at[p, t], s5_s, s5_r, 0, x_at, x_dev),
+         ring_spread(lambda p, t: b_all.at[p, t], s5_s, s5_r, 1, y_at, y_dev), 4)
     a_copy = pltpu.make_async_copy(a_all, a_out, out_sem.at[1])
     b_copy = pltpu.make_async_copy(b_all, b_out, out_sem.at[2])
     a_copy.start()
@@ -531,8 +538,8 @@
             dma, dma, dma, dma, dma((3,)), dma, dma((3,)), dma((3,))]
         + [dma((NZ,))] * 4
         + [dma((steps,))] * 4 + [dma((NZ,))] * 8 + [dma((3,))] * 2 + [dma((steps, NY))] * 4
-        + [dma((4,))] * 2 + [dma((3,))] * 2 + [dma((3,))] * 2 + [dma((4,))] * 2
-        + [dma((2, 3))] * 4 + [dma((NZ,))] * 4 + [dma((2, 3))] * 4,
+        + [dma((4,))] * 2 + [dma((3, 2))] * 2 + [dma((3, 2))] * 2 + [dma((4, 2))] * 2
+        + [dma((2, 3, 3))] * 4 + [dma((NZ,))] * 4 + [dma((2, 3, 4))] * 4,
         compiler_params=pltpu.CompilerParams(
             collective_id=0, has_side_effects=True, vmem_limit_bytes=60 << 20),
         name="layer",

time: 139 us -> 138 us (level)
  no operation moved by 1% of the time
where the time goes in v4:
time: 138 us; the launch traced here: 137 us
  Pallas kernels  136 us (99%)
    pallas_call x1, Pallas kernels, layer(): pl.pallas_call(layer_kernel, out_shape=(jax.ShapeDtypeStruct((2 * BLOCK,...  134 us

profile of v4, /device:TPU:2, one launch (start us, length us, event | category | flops | bytes accessed | tf_op | source)
XLA Modules:
  0.0 137.3 jit_solution(10609823566211445354)
XLA Ops:
  1.3 133.6 %layer.1 = (bf16[256,256]{1,0:T(8,128)(2,1)}, bf16[4,4,3,16,256]{4,3,2,1,0:T(8,128)(2,1)}, bf16[4,4,3,16,256]{4,3,2,1,0:T(8,128)(2,1)}) custom-call(bf16[2,128,256]{2,1,0:T(8,128)(2,1)} %bitcast.7, s32[3,1,64]{2,1,0:T(1,128)} %bitcast.8, s32[1,64]{1,0:T(1,128)} %bitcast.9, s32[1]{0:T(128)} %bitcast.5.count, bf16[64,128,128]{2,1,0:T(8,128)(2,1)} %bitcast.6, ...), custom_call_target="tpu_custom_call" | custom-call | tf_op jit(solution)/shard_map/layer/pallas_call | solution.py:517
  134.9 2.4 %finish.1 = (bf16[256,256]{1,0:T(8,128)(2,1)}, f32[6,256,256]{2,1,0:T(8,128)}) custom-call(bf16[256,256]{1,0:T(8,128)(2,1)} %get-tuple-element.5.result, bf16[4,4,3,16,256]{4,3,2,1,0:T(8,128)(2,1)} %get-tuple-element.6.a_all, bf16[4,4,3,16,256]{4,3,2,1,0:T(8,128)(2,1)} %get-tuple-element.7.b_all), custom_call_target="tpu_custom_call" | custom-call | tf_op jit(solution)/shard_map/finish/pallas_call | solution.py:561

commit v5 on v4

--- a/solution.py
+++ b/solution.py
@@ -27,7 +27,7 @@
 
 TIME_P = [5.0 * k for k in range(FAR + 1)]
 TIME_Q = [5.0 * k + 1.0 for k in range(FAR + 1)]
-TIME_Y = [5.0 * k + 6.0 for k in range(FAR + 1)]
+TIME_Y = [5.0 * k + 6.0 for k in range(FAR)] + [5.0 * FAR + 1.2]
 MESSAGE_LAG = 8.5
 
 
@@ -199,6 +199,13 @@
     pick_copy.start()
     pick_copy.wait()
     y_step(0)
+
+    arrive((0, -1), ROWS_P, ROWS_Q, q0_s.at[0], q0_r.at[0])
+    q_step(1, 3)
+    arrive((0, 1), ROWS_P, ROWS_Q, q0_s.at[1], q0_r.at[1])
+    q_step(1, 1)
+    arrive((0, 2), ROWS_P, ROWS_Q, q0_s.at[2], q0_r.at[2])
+    q_step(1, 2)
 
     lanes = lax.broadcasted_iota(I32, (PARTS, PARTS), 1)
     subs = lax.broadcasted_iota(I32, (PARTS, PARTS), 0)
@@ -233,12 +240,6 @@
     tab[3:4, :] = jnp.where(final < 0, PARTS, final)
     chain[PARTS] = jnp.zeros((BLOCK, D), F32)
 
-    arrive((0, -1), ROWS_P, ROWS_Q, q0_s.at[0], q0_r.at[0])
-    q_step(1, 3)
-    arrive((0, 1), ROWS_P, ROWS_Q, q0_s.at[1], q0_r.at[1])
-    q_step(1, 1)
-    arrive((0, 2), ROWS_P, ROWS_Q, q0_s.at[2], q0_r.at[2])
-    q_step(1, 2)
     tab_copy = pltpu.make_async_copy(tab, tab_s, tab_sem)
     tab_copy.start()
     z_rows[...] = jnp.zeros_like(z_rows)
@@ -326,8 +327,8 @@
         blocks(narrow, 0, 2 * BLOCK)
         if i > 0:
             combine(i - 1)
+        swaps.append(go(remote(give.at[i], ex.at[i], ex_s.at[i], ex_r.at[i], partner)))
         project(panels[i] * 2 + g, keep.at[i])
-        swaps.append(go(remote(give.at[i], ex.at[i], ex_s.at[i], ex_r.at[i], partner)))
     swaps[3].wait_recv()
     own = s * 2 + g
 

time: 138 us -> 137 us (level)
  no operation moved by 1% of the time
where the time goes in v5:
time: 137 us
  Pallas kernels  136 us (99%)
    pallas_call x1, Pallas kernels, layer(): pl.pallas_call(layer_kernel, out_shape=(jax.ShapeDtypeStruct((2 * BLOCK,...  133 us

profile of v5, /device:TPU:2, one launch (start us, length us, event | category | flops | bytes accessed | tf_op | source)
XLA Modules:
  0.0 137.1 jit_solution(535823520185128754)
XLA Ops:
  1.3 133.4 %layer.1 = (bf16[256,256]{1,0:T(8,128)(2,1)}, bf16[4,4,3,16,256]{4,3,2,1,0:T(8,128)(2,1)}, bf16[4,4,3,16,256]{4,3,2,1,0:T(8,128)(2,1)}) custom-call(bf16[2,128,256]{2,1,0:T(8,128)(2,1)} %bitcast.7, s32[3,1,64]{2,1,0:T(1,128)} %bitcast.8, s32[1,64]{1,0:T(1,128)} %bitcast.9, s32[1]{0:T(128)} %bitcast.5.count, bf16[64,128,128]{2,1,0:T(8,128)(2,1)} %bitcast.6, ...), custom_call_target="tpu_custom_call" | custom-call | tf_op jit(solution)/shard_map/layer/pallas_call | solution.py:518
  134.7 2.4 %finish.1 = (bf16[256,256]{1,0:T(8,128)(2,1)}, f32[6,256,256]{2,1,0:T(8,128)}) custom-call(bf16[256,256]{1,0:T(8,128)(2,1)} %get-tuple-element.5.result, bf16[4,4,3,16,256]{4,3,2,1,0:T(8,128)(2,1)} %get-tuple-element.6.a_all, bf16[4,4,3,16,256]{4,3,2,1,0:T(8,128)(2,1)} %get-tuple-element.7.b_all), custom_call_target="tpu_custom_call" | custom-call | tf_op jit(solution)/shard_map/finish/pallas_call | solution.py:562
